TPU v7x, 256 devices: a whole 4x4x8 slice. The times are simulated.
256 devices in a mesh: slab: 64 (over y, x_lo, z), view: 4 (over x_hi, core).
Axes of the slice: x: 4 (x_hi: 2, x_lo: 2; x = x_hi * 2 + x_lo), y: 4, z: 8, core: 2. Of those that a mesh axis runs over, the one named last changes fastest.
Arguments:
- primal: float32 [5, 256, 32, 128], P(None, 'slab', 'view'), may hold values from -6 to 6
- dual: bfloat16 [64, 256, 128], P('view', 'slab'), may hold values from -6 to 6
- footprints: bfloat16 [8, 128, 128], replicated, may hold values from -0.046875 to 0.046875
- tile_index: int32 [64, 8192, 2], P(None, 'slab'), may hold values from 0 to 3
- footprint_offset: int32 [64, 8192, 2], P(None, 'slab'), may hold values from 0 to 7
- w_first: bfloat16 [3, 3, 3, 32, 6], replicated, may hold values from -0.21875 to 0.21875
- w_middle: bfloat16 [3, 3, 3, 32, 32], replicated, may hold values from -0.21875 to 0.21875
- w_last: bfloat16 [3, 3, 3, 5, 32], replicated, may hold values from -0.5 to 0.5
- cotangent: float32 [5, 256, 32, 128], P(None, 'slab', 'view'), may hold values from -6 to 6
Outputs:
- d_primal: float32 [5, 256, 32, 128], P(None, 'slab', 'view')
- d_dual: float32 [64, 256, 128], P('view', 'slab')
- d_first: float32 [3, 3, 3, 32, 6], replicated
- d_middle: float32 [3, 3, 3, 32, 32], replicated
- d_last: float32 [3, 3, 3, 5, 32], replicated
All inputs are finite; a program needn't handle non-finite values.
Results may differ from a plain program's by a relative error of at most 0.0067.
Values may be sent and summed in bfloat16 or wider, within the bound.
No kernel may reach another device: no remote copies, remote signals or barrier semaphores. Data moves between devices by JAX's collectives and lax.ppermute only.
A program may use at most 64 MiB of HBM per device.

v0:
```python
import math
import jax
import jax.numpy as jnp
from jax import lax
from jax.sharding import PartitionSpec as P


def with_halo(cells, sides, width):
    for axis, dim in sides:
        count = lax.axis_size(axis)
        ends = count - 1
        head = lax.slice_in_dim(cells, 0, width, axis=dim)
        tail = lax.slice_in_dim(cells, cells.shape[dim] - width, cells.shape[dim], axis=dim)
        cells = jnp.concatenate(
            [
                lax.ppermute(tail, axis, [(i, (i + 1) % count) for i in range(ends)]),
                cells,
                lax.ppermute(head, axis, [((i + 1) % count, i) for i in range(ends)]),
            ],
            axis=dim,
        )
    return cells


def silu_slope(value):
    sig = jax.nn.sigmoid(value)
    return sig * (1.0 + value * (1.0 - sig))


def flipped(kernel):
    return kernel[::-1, ::-1, ::-1].transpose(0, 1, 2, 4, 3)


def sideways(padded):
    blank = jnp.zeros(padded.shape[:-1] + (1,), padded.dtype)
    left = jnp.concatenate([blank, padded[..., :-1]], axis=-1)
    right = jnp.concatenate([padded[..., 1:], blank], axis=-1)
    return (left, padded, right)


def rims(field):
    return with_halo(field, (("slab", 1), ("view", 2)), 1)


def convolve(parts, kernel, depth, rows):
    total = None
    for za in range(3):
        for yb in range(3):
            for xc in range(3):
                term = jnp.einsum(
                    "oc,czyx->ozyx",
                    kernel[za, yb, xc],
                    parts[xc][:, za : za + depth, yb : yb + rows, :],
                    preferred_element_type=jnp.float32,
                )
                total = term if total is None else total + term
    return total


def kernel_grad(dout, parts, depth, rows):
    terms = []
    for za in range(3):
        for yb in range(3):
            for xc in range(3):
                terms.append(
                    jnp.einsum(
                        "ozyx,czyx->oc",
                        dout,
                        parts[xc][:, za : za + depth, yb : yb + rows, :],
                        preferred_element_type=jnp.float32,
                    )
                )
    return jnp.stack(terms).reshape(3, 3, 3, dout.shape[0], parts[0].shape[0])


def shards(
    primal, dual, footprints, tile_index, footprint_offset, w_first, w_middle, w_last, cotangent
):
    channels, depth, rows_here, width = primal.shape
    views_here, det_tiles, bins = dual.shape
    all_views = tile_index.shape[0]
    taps = tile_index.shape[2]
    foot_count = footprints.shape[0]
    n_view = lax.axis_size("view")
    full_rows = rows_here * n_view
    x_tiles = width // bins
    view_at = lax.axis_index("view")
    forward_mat = footprints.transpose(1, 0, 2).reshape(bins, foot_count * bins)
    backward_mat = footprints.transpose(2, 0, 1).reshape(bins, foot_count * bins)
    tile_grid = tile_index.reshape(all_views, depth, full_rows, x_tiles, taps)
    foot_grid = footprint_offset.reshape(all_views, depth, full_rows, x_tiles, taps)
    stride = det_tiles * foot_count
    heights = jnp.dot(
        dual.reshape(-1, bins), forward_mat, preferred_element_type=jnp.float32
    ).reshape(-1, bins)
    own_tiles = lax.dynamic_slice_in_dim(tile_grid, view_at * views_here, views_here, 0)
    own_foot = lax.dynamic_slice_in_dim(foot_grid, view_at * views_here, views_here, 0)
    count = rows_here * lax.axis_size("view")

    def strip_add_view(view, total):
        picks = view * stride + own_tiles[view] * foot_count + own_foot[view]
        return total + jnp.take(heights, picks, axis=0).sum(axis=3)

    total = lax.fori_loop(
        0, views_here, strip_add_view, jnp.zeros((depth, count, x_tiles, bins), jnp.float32)
    )
    strips = lax.psum_scatter(
        total.reshape(depth, count, width).transpose(1, 0, 2),
        "view",
        scatter_dimension=0,
        tiled=True,
    )
    back = strips.transpose(1, 0, 2)
    x_zero = jnp.concatenate([primal, back[None]], axis=0).astype(jnp.bfloat16)
    g_low = cotangent.astype(jnp.bfloat16)
    x_parts = sideways(with_halo(x_zero, (("slab", 1), ("view", 2)), 1))
    g_parts = sideways(with_halo(g_low, (("slab", 1), ("view", 2)), 1))
    a_one = convolve(x_parts, w_first, depth, rows_here)
    z_one = jax.nn.silu(a_one).astype(jnp.bfloat16)
    z_one_parts = sideways(rims(z_one))
    a_two = convolve(z_one_parts, w_middle, depth, rows_here)
    z_two = jax.nn.silu(a_two).astype(jnp.bfloat16)
    z_two_parts = sideways(rims(z_two))
    dz_two = convolve(g_parts, flipped(w_last), depth, rows_here)
    d_last = kernel_grad(g_low, z_two_parts, depth, rows_here)
    da_two = (dz_two * silu_slope(a_two)).astype(jnp.bfloat16)
    dz_one = convolve(sideways(rims(da_two)), flipped(w_middle), depth, rows_here)
    d_middle = kernel_grad(da_two, z_one_parts, depth, rows_here)
    da_one = (dz_one * silu_slope(a_one)).astype(jnp.bfloat16)
    dx_zero = convolve(sideways(rims(da_one)), flipped(w_first), depth, rows_here)
    d_first = kernel_grad(da_one, x_parts, depth, rows_here)
    d_primal = cotangent + dx_zero[:channels]
    strip_grad = dx_zero[channels].astype(jnp.bfloat16)
    start_grad = jnp.zeros((views_here * det_tiles, bins), jnp.float32)
    piece = lax.all_gather(strip_grad, "view", axis=1, tiled=True)
    count = piece.shape[1]
    proj = jnp.dot(
        piece.reshape(-1, bins), backward_mat, preferred_element_type=jnp.float32
    ).reshape(-1, bins)
    tile_ids = jnp.arange(depth * count * x_tiles, dtype=jnp.int32).reshape(
        depth, count, x_tiles, 1
    )

    def fold_add_view(view, acc):
        source = tile_ids * foot_count + own_foot[view]
        target = view * det_tiles + own_tiles[view]
        return acc + jax.ops.segment_sum(
            jnp.take(proj, source.reshape(-1), axis=0),
            target.reshape(-1),
            num_segments=views_here * det_tiles,
        )

    d_dual = lax.fori_loop(0, views_here, fold_add_view, start_grad).reshape(
        views_here, det_tiles, bins
    )
    summed = lax.psum((d_first, d_middle, d_last), ("slab", "view"))
    scale = 1.0 / math.sqrt(depth * lax.axis_size("slab") * full_rows * width)
    return (d_primal, d_dual, summed[0] * scale, summed[1] * scale, summed[2] * scale)


def solution(mesh):
    placed = (
        P(None, "slab", "view", None),
        P("view", "slab", None),
        P(),
        P(None, "slab", None),
        P(None, "slab", None),
        P(),
        P(),
        P(),
        P(None, "slab", "view", None),
    )
    return jax.shard_map(
        shards,
        mesh=mesh,
        in_specs=placed,
        out_specs=(P(None, "slab", "view", None), P("view", "slab", None), P(), P(), P()),
        check_vma=False,
    )
```

profile of v0, /device:TPU:1, one launch (start us, length us, event | category | flops | bytes accessed | tf_op | source)
XLA Modules:
  0.0 618.3 jit_solution(12563308730298618970)
XLA Ops:
  7.3 3.5 copy.388
  10.8 2.7 copy.389
  15.7 21.8 %while.30 = (s32[]{:T(128)}, f32[4,32,1,128]{3,2,1,0:T(1,128)S(1)}, s32[16,4,32,1,2]{4,2,1,3,0:T(8,128)S(1)}, s32[16,4,32,1,2]{4,2,1,3,0:T(8,128)S(1)}, f32[512,...) while((s32[]{:T(128)}, f32[4,32,1,128]{3,2,1,0:T(1,128)S(1)}, ...), condition=%wide.region_2.3_spmd.clone, body=%wide.region_0.2_spmd.clone.sunk | while | flops 86788 | bytes 669307 | solution.py:104
  38.3 4.4 collective-permute-start
  47.3 6.5 %collective-permute-start.2 = (bf16[5,6,1,128]{3,2,1,0:T(2,128)(2,1)S(1)}, bf16[5,6,1,128]{3,2,1,0:T(2,128)(2,1)S(1)}, u32[]{:S(2)}, u32[]{:S(2)}) collective-permute-start(bf16[5,6,1,128]{3,2,1,0:T(2,128)(2,1)S(1)} %get-tuple-element.443), channel_id=1, source_target_pairs={{0,1},{1,2},{2,3},{4,5},{5,6},{6,7},{8,9},{9,10},{10,11},{12,13},{... | collective-permute-start | bytes 23048 | tf_op jit(solution)/shard_map/ppermute | solution.py:16
  55.7 4.6 collective-permute-done.3
  68.7 4.5 reduce-scatter.2.cloned.1.call-done
  73.9 3.2 collective-permute-start.4
  81.5 4.7 collective-permute-start.6
  88.3 4.6 collective-permute-done.7
  106.4 3.2 collective-permute-start.8
  112.3 2.8 collective-permute-done.9
  115.2 3.1 collective-permute-start.10
  120.3 4.9 collective-permute-done.11
  158.0 4.8 collective-permute-start.20
  164.1 4.3 collective-permute-start.12
  169.7 240.3 %all-reduce.15.cloned.1.call-done = f32[3,3,3,32,32]{4,3,2,1,0:T(8,128)} async-done(((f32[3,3,3,32,32]{4,3,2,1,0:T(8,128)}), f32[3,3,3,32,32]{4,3,2,1,0:T(8,128)}) %all-reduce.15.cloned.1.call-update) | async-done | bytes 110608 | tf_op jit(solution)/shard_map/psum | solution.py:156
  411.8 5.5 collective-permute-start.22
  419.3 5.1 collective-permute-start.14
  426.6 4.8 collective-permute-done.15
  453.8 80.9 %all-reduce.12 = (f32[3,3,3,32,6]{3,4,2,1,0:T(8,128)S(1)}, f32[3,3,3,5,32]{4,2,3,1,0:T(4,128)S(1)}) all-reduce(f32[3,3,3,32,6]{3,4,2,1,0:T(8,128)} %bitcast.1969, f32[3,3,3,5,32]{4,2,3,1,0:T(4,128)S(1)} %copy.582), channel_id=1, replica_groups=mesh['slab'=64,'view'=4] {'slab','view'}, use_global_device_ids=true, to_apply=%region_7.8 | all-reduce | flops 9504 | bytes 76032 | tf_op jit(solution)/shard_map/psum | solution.py:156
  535.4 3.8 collective-permute-start.18
  542.0 4.1 collective-permute-done.19
  551.5 5.6 all-gather
  557.4 53.1 %while.29 = (s32[]{:T(128)}, f32[64,128]{1,0:T(8,128)S(1)}, s32[16,4,32,1,2]{4,2,1,3,0:T(8,128)S(1)}, s32[16,4,32,1,2]{4,2,1,3,0:T(8,128)S(1)}, f32[1024,128]{1,...) while((s32[]{:T(128)}, f32[64,128]{1,0:T(8,128)S(1)}, ...), condition=%wide.region_6.7_spmd.clone.clone, body=%wide.region_4.6_spmd.clone.clone.sunk | while | flops 70019 | bytes 588653 | solution.py:153
  561.6 2.4 scatter_custom_fusion.6
  565.0 2.4 scatter_custom_fusion.6
  578.2 2.4 scatter_custom_fusion.6
  581.5 2.4 scatter_custom_fusion.6
  584.9 2.4 scatter_custom_fusion.6
  591.5 2.4 scatter_custom_fusion.6
  601.4 2.4 scatter_custom_fusion.6
  (743 shorter events, 171.2 us)
Async XLA Ops:
  7.2 66.0 %reduce-scatter.2.cloned.1.call-start = ((), (), s32[]{:S(2)}) async-start(), calls=%async_computation.1 | async-start | bytes 81920 | tf_op jit(solution)/shard_map/reduce_scatter | solution.py:107
  15.7 28.2 %copy-start.58 = (bf16[3,3,3,5,32]{4,2,3,1,0:T(4,128)(2,1)S(1)}, bf16[3,3,3,5,32]{4,2,3,1,0:T(4,128)(2,1)}, u32[]{:S(2)}) copy-start(bf16[3,3,3,5,32]{4,2,3,1,0:T(4,128)(2,1)} %param.20) | copy-start | bytes 25924
  15.7 28.3 %copy-start.5 = (bf16[3,3,3,32,32]{4,3,2,1,0:T(8,128)(2,1)S(1)}, bf16[3,3,3,32,32]{4,3,2,1,0:T(8,128)(2,1)}, u32[]{:S(2)}) copy-start(bf16[3,3,3,32,32]{4,3,2,1,0:T(8,128)(2,1)} %param.19) | copy-start | bytes 165892
  15.7 28.5 %copy-start.49 = (bf16[3,3,3,32,6]{3,4,2,1,0:T(8,128)(2,1)S(1)}, bf16[3,3,3,32,6]{3,4,2,1,0:T(8,128)(2,1)}, u32[]{:S(2)}) copy-start(bf16[3,3,3,32,6]{3,4,2,1,0:T(8,128)(2,1)} %param.18) | copy-start | bytes 31108
  15.7 29.1 %copy-start.54 = (f32[5,4,8,128]{3,2,1,0:T(8,128)S(1)}, f32[5,4,8,128]{3,2,1,0:T(8,128)}, u32[]{:S(2)}) copy-start(f32[5,4,8,128]{3,2,1,0:T(8,128)} %param.13) | copy-start | bytes 245764
  38.2 371.8 %all-reduce.15.cloned.1.call-start = ((), (), s32[]{:S(2)}) async-start(), calls=%async_computation.2 | async-start | bytes 884736 | tf_op jit(solution)/shard_map/psum | solution.py:156
  38.3 6.6 %collective-permute-start = (bf16[5,1,8,128]{3,2,1,0:T(8,128)(2,1)S(1)}, bf16[5,1,8,128]{3,2,1,0:T(8,128)(2,1)S(1)}, u32[]{:S(2)}, u32[]{:S(2)}) collective-permute-start(bf16[5,1,8,128]{3,2,1,0:T(8,128)(2,1)S(1)} %get-tuple-element.452), channel_id=1, source_target_pairs={{0,4},{4,8},{8,12},{12,16},{16,20},{20,24},{24,28},{28,32},{32,36}... | collective-permute-start | bytes 30728 | tf_op jit(solution)/shard_map/ppermute | solution.py:16
  42.6 4.6 collective-permute-start.1
  44.0 23.4 %copy-start.51 = (bf16[3,3,3,32,5]{3,4,2,1,0:T(8,128)(2,1)}, bf16[3,3,3,32,5]{3,4,2,1,0:T(8,128)(2,1)S(1)}, u32[]{:S(2)}) copy-start(bf16[3,3,3,32,5]{3,4,2,1,0:T(8,128)(2,1)S(1)} %reverse_bitcast_fusion.2) | copy-start | bytes 25924
  47.3 8.4 %collective-permute-start.2 = (bf16[5,6,1,128]{3,2,1,0:T(2,128)(2,1)S(1)}, bf16[5,6,1,128]{3,2,1,0:T(2,128)(2,1)S(1)}, u32[]{:S(2)}, u32[]{:S(2)}) collective-permute-start(bf16[5,6,1,128]{3,2,1,0:T(2,128)(2,1)S(1)} %get-tuple-element.443), channel_id=1, source_target_pairs={{0,1},{1,2},{2,3},{4,5},{5,6},{6,7},{8,9},{9,10},{10,11},{12,13},{... | collective-permute-start | bytes 23048 | tf_op jit(solution)/shard_map/ppermute | solution.py:16
  53.7 6.6 %collective-permute-start.3 = (bf16[5,6,1,128]{3,2,1,0:T(2,128)(2,1)S(1)}, bf16[5,6,1,128]{3,2,1,0:T(2,128)(2,1)S(1)}, u32[]{:S(2)}, u32[]{:S(2)}) collective-permute-start(bf16[5,6,1,128]{3,2,1,0:T(2,128)(2,1)S(1)} %get-tuple-element.444), channel_id=1, source_target_pairs={{1,0},{2,1},{3,2},{5,4},{6,5},{7,6},{9,8},{10,9},{11,10},{13,12},{... | collective-permute-start | bytes 23048 | tf_op jit(solution)/shard_map/ppermute | solution.py:18
  73.9 5.5 collective-permute-start.4
  77.1 4.4 collective-permute-start.5
  81.5 6.7 %collective-permute-start.6 = (bf16[6,6,1,128]{3,2,1,0:T(2,128)(2,1)S(1)}, bf16[6,6,1,128]{3,2,1,0:T(2,128)(2,1)S(1)}, u32[]{:S(2)}, u32[]{:S(2)}) collective-permute-start(bf16[6,6,1,128]{3,2,1,0:T(2,128)(2,1)S(1)} %get-tuple-element.440), channel_id=1, source_target_pairs={{0,1},{1,2},{2,3},{4,5},{5,6},{6,7},{8,9},{9,10},{10,11},{12,13},{... | collective-permute-start | bytes 27656 | tf_op jit(solution)/shard_map/ppermute | solution.py:16
  86.3 6.6 %collective-permute-start.7 = (bf16[6,6,1,128]{3,2,1,0:T(2,128)(2,1)S(1)}, bf16[6,6,1,128]{3,2,1,0:T(2,128)(2,1)S(1)}, u32[]{:S(2)}, u32[]{:S(2)}) collective-permute-start(bf16[6,6,1,128]{3,2,1,0:T(2,128)(2,1)S(1)} %get-tuple-element.439), channel_id=1, source_target_pairs={{1,0},{2,1},{3,2},{5,4},{6,5},{7,6},{9,8},{10,9},{11,10},{13,12},{... | collective-permute-start | bytes 27656 | tf_op jit(solution)/shard_map/ppermute | solution.py:18
  106.4 5.9 collective-permute-start.8
  109.6 5.6 collective-permute-start.9
  115.2 5.1 collective-permute-start.10
  118.3 6.9 %collective-permute-start.11 = (bf16[32,6,1,128]{3,0,2,1:T(8,128)(2,1)S(1)}, bf16[32,6,1,128]{3,0,2,1:T(8,128)(2,1)S(1)}, u32[]{:S(2)}, u32[]{:S(2)}) collective-permute-start(bf16[32,6,1,128]{3,0,2,1:T(8,128)(2,1)S(1)} %get-tuple-element.372), channel_id=1, source_target_pairs={{1,0},{2,1},{3,2},{5,4},{6,5},{7,6},{9,8},{10,9},{11,10},{13,12},{... | collective-permute-start | bytes 147464 | tf_op jit(solution)/shard_map/ppermute | solution.py:18
  158.0 253.8 %collective-permute-start.20 = (bf16[32,1,8,128]{3,0,2,1:T(8,128)(2,1)}, bf16[32,1,8,128]{3,0,2,1:T(8,128)(2,1)S(1)}, u32[]{:S(2)}, u32[]{:S(2)}) collective-permute-start(bf16[32,1,8,128]{3,0,2,1:T(8,128)(2,1)} %get-tuple-element.375), channel_id=1, source_target_pairs={{0,4},{4,8},{8,12},{12,16},{16,20},{20,24},{24,28},{28,32},{32,36}... | collective-permute-start | bytes 196616 | tf_op jit(solution)/shard_map/ppermute | solution.py:16
  162.8 249.0 %collective-permute-start.21 = (bf16[32,1,8,128]{3,0,2,1:T(8,128)(2,1)}, bf16[32,1,8,128]{3,0,2,1:T(8,128)(2,1)S(1)}, u32[]{:S(2)}, u32[]{:S(2)}) collective-permute-start(bf16[32,1,8,128]{3,0,2,1:T(8,128)(2,1)} %get-tuple-element.376), channel_id=1, source_target_pairs={{4,0},{8,4},{12,8},{16,12},{20,16},{24,20},{28,24},{32,28},{36,32}... | collective-permute-start | bytes 196616 | tf_op jit(solution)/shard_map/ppermute | solution.py:18
  164.1 255.2 %collective-permute-start.12 = (bf16[32,1,8,128]{3,0,2,1:T(8,128)(2,1)}, bf16[32,1,8,128]{3,0,2,1:T(8,128)(2,1)S(1)}, u32[]{:S(2)}, u32[]{:S(2)}) collective-permute-start(bf16[32,1,8,128]{3,0,2,1:T(8,128)(2,1)} %get-tuple-element.379), channel_id=1, source_target_pairs={{0,4},{4,8},{8,12},{12,16},{16,20},{20,24},{24,28},{28,32},{32,36}... | collective-permute-start | bytes 196616 | tf_op jit(solution)/shard_map/ppermute | solution.py:16
  168.4 250.9 %collective-permute-start.13 = (bf16[32,1,8,128]{3,0,2,1:T(8,128)(2,1)}, bf16[32,1,8,128]{3,0,2,1:T(8,128)(2,1)S(1)}, u32[]{:S(2)}, u32[]{:S(2)}) collective-permute-start(bf16[32,1,8,128]{3,0,2,1:T(8,128)(2,1)} %get-tuple-element.380), channel_id=1, source_target_pairs={{4,0},{8,4},{12,8},{16,12},{20,16},{24,20},{28,24},{32,28},{36,32}... | collective-permute-start | bytes 196616 | tf_op jit(solution)/shard_map/ppermute | solution.py:18
  411.8 27.3 %collective-permute-start.22 = (bf16[32,6,1,128]{3,0,2,1:T(8,128)(2,1)S(1)}, bf16[32,6,1,128]{3,0,2,1:T(8,128)(2,1)S(1)}, u32[]{:S(2)}, u32[]{:S(2)}) collective-permute-start(bf16[32,6,1,128]{3,0,2,1:T(8,128)(2,1)S(1)} %get-tuple-element.361), channel_id=1, source_target_pairs={{0,1},{1,2},{2,3},{4,5},{5,6},{6,7},{8,9},{9,10},{10,11},{12,13},{... | collective-permute-start | bytes 147464 | tf_op jit(solution)/shard_map/ppermute | solution.py:16
  417.3 21.8 %collective-permute-start.23 = (bf16[32,6,1,128]{3,0,2,1:T(8,128)(2,1)S(1)}, bf16[32,6,1,128]{3,0,2,1:T(8,128)(2,1)S(1)}, u32[]{:S(2)}, u32[]{:S(2)}) collective-permute-start(bf16[32,6,1,128]{3,0,2,1:T(8,128)(2,1)S(1)} %get-tuple-element.362), channel_id=1, source_target_pairs={{1,0},{2,1},{3,2},{5,4},{6,5},{7,6},{9,8},{10,9},{11,10},{13,12},{... | collective-permute-start | bytes 147464 | tf_op jit(solution)/shard_map/ppermute | solution.py:18
  419.3 7.3 %collective-permute-start.14 = (bf16[32,6,1,128]{3,0,2,1:T(8,128)(2,1)S(1)}, bf16[32,6,1,128]{3,0,2,1:T(8,128)(2,1)S(1)}, u32[]{:S(2)}, u32[]{:S(2)}) collective-permute-start(bf16[32,6,1,128]{3,0,2,1:T(8,128)(2,1)S(1)} %get-tuple-element.367), channel_id=1, source_target_pairs={{0,1},{1,2},{2,3},{4,5},{5,6},{6,7},{8,9},{9,10},{10,11},{12,13},{... | collective-permute-start | bytes 147464 | tf_op jit(solution)/shard_map/ppermute | solution.py:16
  424.5 6.9 %collective-permute-start.15 = (bf16[32,6,1,128]{3,0,2,1:T(8,128)(2,1)S(1)}, bf16[32,6,1,128]{3,0,2,1:T(8,128)(2,1)S(1)}, u32[]{:S(2)}, u32[]{:S(2)}) collective-permute-start(bf16[32,6,1,128]{3,0,2,1:T(8,128)(2,1)S(1)} %get-tuple-element.368), channel_id=1, source_target_pairs={{1,0},{2,1},{3,2},{5,4},{6,5},{7,6},{9,8},{10,9},{11,10},{13,12},{... | collective-permute-start | bytes 147464 | tf_op jit(solution)/shard_map/ppermute | solution.py:18
  450.9 84.4 %collective-permute-start.16 = (bf16[32,1,8,128]{3,0,2,1:T(8,128)(2,1)}, bf16[32,1,8,128]{3,0,2,1:T(8,128)(2,1)S(1)}, u32[]{:S(2)}, u32[]{:S(2)}) collective-permute-start(bf16[32,1,8,128]{3,0,2,1:T(8,128)(2,1)} %get-tuple-element.377), channel_id=1, source_target_pairs={{0,4},{4,8},{8,12},{12,16},{16,20},{20,24},{24,28},{28,32},{32,36}... | collective-permute-start | bytes 196616 | tf_op jit(solution)/shard_map/ppermute | solution.py:16
  452.3 83.0 %collective-permute-start.17 = (bf16[32,1,8,128]{3,0,2,1:T(8,128)(2,1)}, bf16[32,1,8,128]{3,0,2,1:T(8,128)(2,1)S(1)}, u32[]{:S(2)}, u32[]{:S(2)}) collective-permute-start(bf16[32,1,8,128]{3,0,2,1:T(8,128)(2,1)} %get-tuple-element.378), channel_id=1, source_target_pairs={{4,0},{8,4},{12,8},{16,12},{20,16},{24,20},{28,24},{32,28},{36,32}... | collective-permute-start | bytes 196616 | tf_op jit(solution)/shard_map/ppermute | solution.py:18
  535.4 6.6 %collective-permute-start.18 = (bf16[32,6,1,128]{3,0,2,1:T(8,128)(2,1)S(1)}, bf16[32,6,1,128]{3,0,2,1:T(8,128)(2,1)S(1)}, u32[]{:S(2)}, u32[]{:S(2)}) collective-permute-start(bf16[32,6,1,128]{3,0,2,1:T(8,128)(2,1)S(1)} %get-tuple-element.363), channel_id=1, source_target_pairs={{0,1},{1,2},{2,3},{4,5},{5,6},{6,7},{8,9},{9,10},{10,11},{12,13},{... | collective-permute-start | bytes 147464 | tf_op jit(solution)/shard_map/ppermute | solution.py:16
  539.2 6.9 %collective-permute-start.19 = (bf16[32,6,1,128]{3,0,2,1:T(8,128)(2,1)S(1)}, bf16[32,6,1,128]{3,0,2,1:T(8,128)(2,1)S(1)}, u32[]{:S(2)}, u32[]{:S(2)}) collective-permute-start(bf16[32,6,1,128]{3,0,2,1:T(8,128)(2,1)S(1)} %get-tuple-element.364), channel_id=1, source_target_pairs={{1,0},{2,1},{3,2},{5,4},{6,5},{7,6},{9,8},{10,9},{11,10},{13,12},{... | collective-permute-start | bytes 147464 | tf_op jit(solution)/shard_map/ppermute | solution.py:18
  557.1 54.1 %copy-start.1 = (bf16[16,4,128]{2,1,0:T(4,128)(2,1)S(1)}, bf16[16,4,128]{2,1,0:T(4,128)(2,1)}, u32[]{:S(2)}) copy-start(bf16[16,4,128]{2,1,0:T(4,128)(2,1)} %param.14) | copy-start | bytes 49156
  (56 other events, 319.5 us)
Sparse Core Ops, SparseCore 0:
  38.3 34.8 reduce-scatter.1
  157.4 252.5 all-reduce.14
where the time goes:
time: 628 us; the launch traced here: 618 us
  waiting for transfers between devices  275 us (44%)
  blocking collectives  86.5 us (14%)
  matrix products  72.4 us (12%)
  starting transfers between devices  70.2 us (11%)
  other arithmetic  51.7 us (8%)
  local copies, waits for them, and re-layouts  44 us (7%)
  between operations  16.3 us (3%)
    psum x1, waiting for transfers between devices, shards(): summed = lax.psum((d_first, d_middle, d_last), ('slab', 'view'))  240 us
    psum x1, blocking collectives, shards(): summed = lax.psum((d_first, d_middle, d_last), ('slab', 'view'))  80.9 us
    ppermute x12, starting transfers between devices, with_halo(): lax.ppermute(tail, axis, [(i, (i + 1) % count) for i in range(ends)])  50 us
    dot_general x135, matrix products, convolve(): jnp.einsum('oc,czyx->ozyx', kernel[za, yb, xc], parts[xc][:, za:za + dept...  40 us
    scatter-add x16, other arithmetic, fold_add_view(): jax.ops.segment_sum(jnp.take(proj, source.reshape(-1), axis=0), target.re...  38.8 us
    dot_general x81, matrix products, kernel_grad(): jnp.einsum('ozyx,czyx->oc', dout, parts[xc][:, za:za + depth, yb:yb + row...  31.9 us
    ppermute x12, waiting for transfers between devices, with_halo(): lax.ppermute(head, axis, [((i + 1) % count, i) for i in range(ends)])  30.4 us
    ppermute x12, starting transfers between devices, with_halo(): lax.ppermute(head, axis, [((i + 1) % count, i) for i in range(ends)])  20.1 us
  transfers between devices with their start and end apart: 26, of which 10 were waited for; matrix products, arithmetic and copies ran while one was open for 4% of the time, Pallas kernels for 0%

commit v1 on v0

--- a/solution.py
+++ b/solution.py
@@ -153,7 +153,9 @@
     d_dual = lax.fori_loop(0, views_here, fold_add_view, start_grad).reshape(
         views_here, det_tiles, bins
     )
-    summed = lax.psum((d_first, d_middle, d_last), ("slab", "view"))
+    summed = (d_first, d_middle, d_last)
+    for tick in ("slab", "view"):
+        summed = lax.psum(summed, axis_name=tick)
     scale = 1.0 / math.sqrt(depth * lax.axis_size("slab") * full_rows * width)
     return (d_primal, d_dual, summed[0] * scale, summed[1] * scale, summed[2] * scale)
 

time: 628 us -> 1220 us (1.94)
  waiting for transfers between devices: 275 us -> 564 us
  blocking collectives: 86.5 us -> 371 us
  matrix products: 72.4 us -> 87.1 us
    psum x1 -> x2, waiting for transfers between devices: 240 us -> 530 us  [shards(): summed = lax.psum(summed, axis_name=tick)]
    psum x1 -> x2, blocking collectives: 80.9 us -> 365 us  [shards(): summed = lax.psum(summed, axis_name=tick)]
    dot_general x81, matrix products: 31.9 us -> 48 us  [kernel_grad(): jnp.einsum('ozyx,czyx->oc', dout, parts[xc][:, za:za + depth, yb:yb + row...]
  transfers between devices with their start and end apart: 26 -> 27, of which waited for: 10 -> 10; matrix products, arithmetic and copies ran while one was open for 4% -> 5% of each run, Pallas kernels for 0% -> 0%
where the time goes in v1:
time: 1220 us; the launch traced here: 1210 us
  waiting for transfers between devices  564 us (46%)
  blocking collectives  371 us (30%)
  matrix products  87.1 us (7%)
  starting transfers between devices  69.1 us (6%)
  other arithmetic  57.1 us (5%)
  local copies, waits for them, and re-layouts  44 us (4%)
  between operations  16.1 us (1%)
    psum x2, waiting for transfers between devices, shards(): summed = lax.psum(summed, axis_name=tick)  530 us
    psum x2, blocking collectives, shards(): summed = lax.psum(summed, axis_name=tick)  365 us
    ppermute x12, starting transfers between devices, with_halo(): lax.ppermute(tail, axis, [(i, (i + 1) % count) for i in range(ends)])  48.3 us
    dot_general x81, matrix products, kernel_grad(): jnp.einsum('ozyx,czyx->oc', dout, parts[xc][:, za:za + depth, yb:yb + row...  48 us
    scatter-add x16, other arithmetic, fold_add_view(): jax.ops.segment_sum(jnp.take(proj, source.reshape(-1), axis=0), target.re...  38.8 us
    dot_general x135, matrix products, convolve(): jnp.einsum('oc,czyx->ozyx', kernel[za, yb, xc], parts[xc][:, za:za + dept...  38.6 us
    ppermute x12, waiting for transfers between devices, with_halo(): lax.ppermute(head, axis, [((i + 1) % count, i) for i in range(ends)])  28.5 us
  transfers between devices with their start and end apart: 27, of which 10 were waited for; matrix products, arithmetic and copies ran while one was open for 5% of the time, Pallas kernels for 0%

profile of v1, /device:TPU:1, one launch (start us, length us, event | category | flops | bytes accessed | tf_op | source)
XLA Modules:
  0.0 1209.4 jit_solution(12824381290203328585)
XLA Ops:
  7.3 3.5 copy.388
  10.8 2.7 copy.389
  15.8 21.8 %while.30 = (s32[]{:T(128)}, f32[4,32,1,128]{3,2,1,0:T(1,128)S(1)}, s32[16,4,32,1,2]{4,2,1,3,0:T(8,128)S(1)}, s32[16,4,32,1,2]{4,2,1,3,0:T(8,128)S(1)}, f32[512,...) while((s32[]{:T(128)}, f32[4,32,1,128]{3,2,1,0:T(1,128)S(1)}, ...), condition=%wide.region_2.3_spmd.clone, body=%wide.region_0.2_spmd.clone.sunk | while | flops 86788 | bytes 669307 | solution.py:104
  38.3 4.4 collective-permute-start
  47.3 6.5 collective-permute-start.2
  55.7 4.6 collective-permute-done.3
  68.0 5.2 reduce-scatter.2.cloned.1.call-done
  73.9 3.2 collective-permute-start.4
  78.7 2.8 collective-permute-done.5
  81.6 4.7 collective-permute-start.6
  88.3 4.6 collective-permute-done.7
  106.4 3.2 collective-permute-start.8
  112.4 2.8 collective-permute-done.9
  115.2 3.1 collective-permute-start.10
  120.3 4.9 collective-permute-done.11
  154.0 4.8 collective-permute-start.20
  164.2 4.3 collective-permute-start.12
  170.4 2.4 collective-permute-start.22
  172.9 2.5 collective-permute-start.23
  176.1 4.6 collective-permute-start.14
  183.6 529.7 %all-reduce.17.cloned.1.call-done = f32[3,3,3,32,32]{4,3,2,1,0:T(8,128)} async-done(((f32[3,3,3,32,32]{4,3,2,1,0:T(8,128)}), f32[3,3,3,32,32]{4,3,2,1,0:T(8,128)}) %all-reduce.17.cloned.1.call-update) | async-done | bytes 110608 | tf_op jit(solution)/shard_map/psum | solution.py:158
  752.3 252.6 %all-reduce.12 = (f32[3,3,3,32,6]{3,4,2,1,0:T(8,128)S(1)}, f32[3,3,3,5,32]{4,2,3,1,0:T(4,128)S(1)}) all-reduce(f32[3,3,3,32,6]{3,4,2,1,0:T(8,128)} %bitcast.559, f32[3,3,3,5,32]{4,2,3,1,0:T(4,128)S(1)} %copy.582), channel_id=1, replica_groups=mesh['slab'=64,'view'=4] {'slab'}, use_global_device_ids=true, to_apply=%region_7.8 | all-reduce | flops 9504 | bytes 76032 | tf_op jit(solution)/shard_map/psum | solution.py:158
  1004.9 112.4 %all-reduce.13 = (f32[3,3,3,32,6]{3,4,2,1,0:T(8,128)S(1)}, f32[3,3,3,5,32]{4,2,3,1,0:T(4,128)S(1)}) all-reduce(f32[3,3,3,32,6]{3,4,2,1,0:T(8,128)S(1)} %get-tuple-element.299, f32[3,3,3,5,32]{4,2,3,1,0:T(4,128)S(1)} %get-tuple-element.300), channel_id=1, replica_groups=mesh['slab'=64,'view'=4] {'view'}, use_global_device_ids=true, to_apply=%region_8.9 | all-reduce | flops 9504 | bytes 76032 | tf_op jit(solution)/shard_map/psum | solution.py:158
  1121.4 3.4 collective-permute-done.17
  1124.8 5.9 collective-permute-start.18
  1134.7 2.9 collective-permute-done.19
  1143.0 5.6 all-gather
  1148.9 53.1 %while.29 = (s32[]{:T(128)}, f32[64,128]{1,0:T(8,128)S(1)}, s32[16,4,32,1,2]{4,2,1,3,0:T(8,128)S(1)}, s32[16,4,32,1,2]{4,2,1,3,0:T(8,128)S(1)}, f32[1024,128]{1,...) while((s32[]{:T(128)}, f32[64,128]{1,0:T(8,128)S(1)}, ...), condition=%wide.region_6.7_spmd.clone.clone, body=%wide.region_4.6_spmd.clone.clone.sunk | while | flops 70019 | bytes 588653 | solution.py:153
  1153.1 2.4 scatter_custom_fusion.6
  1156.5 2.4 scatter_custom_fusion.6
  1169.7 2.4 scatter_custom_fusion.6
  1176.3 2.4 scatter_custom_fusion.6
  (751 shorter events, 194.4 us)
Async XLA Ops:
  7.2 66.0 %reduce-scatter.2.cloned.1.call-start = ((), (), s32[]{:S(2)}) async-start(), calls=%async_computation.1 | async-start | bytes 81920 | tf_op jit(solution)/shard_map/reduce_scatter | solution.py:107
  15.8 29.1 %copy-start.55 = (f32[5,4,8,128]{3,2,1,0:T(8,128)S(1)}, f32[5,4,8,128]{3,2,1,0:T(8,128)}, u32[]{:S(2)}) copy-start(f32[5,4,8,128]{3,2,1,0:T(8,128)} %param.13) | copy-start | bytes 245764
  38.2 675.1 %all-reduce.17.cloned.1.call-start = ((), (), s32[]{:S(2)}) async-start(), calls=%async_computation.2 | async-start | bytes 884736 | tf_op jit(solution)/shard_map/psum | solution.py:158
  38.3 6.6 collective-permute-start
  42.7 4.6 collective-permute-start.1
  44.0 34.4 %copy-start.53 = (bf16[3,3,3,32,5]{3,4,2,1,0:T(8,128)(2,1)}, bf16[3,3,3,32,5]{3,4,2,1,0:T(8,128)(2,1)S(1)}, u32[]{:S(2)}) copy-start(bf16[3,3,3,32,5]{3,4,2,1,0:T(8,128)(2,1)S(1)} %reverse_bitcast_fusion.2) | copy-start | bytes 25924
  47.3 8.4 collective-permute-start.2
  53.8 6.6 collective-permute-start.3
  73.9 4.8 collective-permute-start.4
  77.1 4.4 collective-permute-start.5
  81.6 6.7 collective-permute-start.6
  86.3 6.6 collective-permute-start.7
  106.4 5.9 collective-permute-start.8
  109.6 5.6 collective-permute-start.9
  115.2 5.1 collective-permute-start.10
  118.3 6.9 collective-permute-start.11
  154.0 15.7 %collective-permute-start.20 = (bf16[32,1,8,128]{3,0,2,1:T(8,128)(2,1)}, bf16[32,1,8,128]{3,0,2,1:T(8,128)(2,1)S(1)}, u32[]{:S(2)}, u32[]{:S(2)}) collective-permute-start(bf16[32,1,8,128]{3,0,2,1:T(8,128)(2,1)} %get-tuple-element.377), channel_id=1, source_target_pairs={{0,4},{4,8},{8,12},{12,16},{16,20},{20,24},{24,28},{28,32},{32,36}... | collective-permute-start | bytes 196616 | tf_op jit(solution)/shard_map/ppermute | solution.py:16
  158.9 10.9 collective-permute-start.21
  164.1 968.7 %all-reduce.19.cloned.1.call-start = ((), (), s32[]{:S(2)}) async-start(), calls=%async_computation.3 | async-start | bytes 884736 | tf_op jit(solution)/shard_map/psum | solution.py:158
  164.2 11.2 collective-permute-start.12
  168.5 6.9 collective-permute-start.13
  170.4 552.9 %collective-permute-start.22 = (bf16[32,6,1,128]{3,0,2,1:T(8,128)(2,1)}, bf16[32,6,1,128]{3,0,2,1:T(8,128)(2,1)}, u32[]{:S(2)}, u32[]{:S(2)}) collective-permute-start(bf16[32,6,1,128]{3,0,2,1:T(8,128)(2,1)} %get-tuple-element.363), channel_id=1, source_target_pairs={{0,1},{1,2},{2,3},{4,5},{5,6},{6,7},{8,9},{9,10},{10,11},{12,13},{... | collective-permute-start | bytes 147464 | tf_op jit(solution)/shard_map/ppermute | solution.py:16
  172.9 550.5 %collective-permute-start.23 = (bf16[32,6,1,128]{3,0,2,1:T(8,128)(2,1)}, bf16[32,6,1,128]{3,0,2,1:T(8,128)(2,1)}, u32[]{:S(2)}, u32[]{:S(2)}) collective-permute-start(bf16[32,6,1,128]{3,0,2,1:T(8,128)(2,1)} %get-tuple-element.364), channel_id=1, source_target_pairs={{1,0},{2,1},{3,2},{5,4},{6,5},{7,6},{9,8},{10,9},{11,10},{13,12},{... | collective-permute-start | bytes 147464 | tf_op jit(solution)/shard_map/ppermute | solution.py:18
  176.1 537.3 %collective-permute-start.14 = (bf16[32,6,1,128]{3,0,2,1:T(8,128)(2,1)}, bf16[32,6,1,128]{3,0,2,1:T(8,128)(2,1)}, u32[]{:S(2)}, u32[]{:S(2)}) collective-permute-start(bf16[32,6,1,128]{3,0,2,1:T(8,128)(2,1)} %get-tuple-element.369), channel_id=1, source_target_pairs={{0,1},{1,2},{2,3},{4,5},{5,6},{6,7},{8,9},{9,10},{10,11},{12,13},{... | collective-permute-start | bytes 147464 | tf_op jit(solution)/shard_map/ppermute | solution.py:16
  180.6 532.7 %collective-permute-start.15 = (bf16[32,6,1,128]{3,0,2,1:T(8,128)(2,1)}, bf16[32,6,1,128]{3,0,2,1:T(8,128)(2,1)}, u32[]{:S(2)}, u32[]{:S(2)}) collective-permute-start(bf16[32,6,1,128]{3,0,2,1:T(8,128)(2,1)} %get-tuple-element.370), channel_id=1, source_target_pairs={{1,0},{2,1},{3,2},{5,4},{6,5},{7,6},{9,8},{10,9},{11,10},{13,12},{... | collective-permute-start | bytes 147464 | tf_op jit(solution)/shard_map/ppermute | solution.py:18
  737.4 381.8 %copy-start.57 = (bf16[32,1,8,128]{3,0,2,1:T(8,128)(2,1)S(1)}, bf16[32,1,8,128]{3,0,2,1:T(8,128)(2,1)}, u32[]{:S(2)}) copy-start(bf16[32,1,8,128]{3,0,2,1:T(8,128)(2,1)} %get-tuple-element.380) | copy-start | bytes 196612
  737.4 383.1 %copy-start.54 = (bf16[3,3,3,6,32]{4,3,2,1,0:T(8,128)(2,1)S(1)}, bf16[3,3,3,6,32]{4,3,2,1,0:T(8,128)(2,1)}, u32[]{:S(2)}) copy-start(bf16[3,3,3,6,32]{4,3,2,1,0:T(8,128)(2,1)} %reverse_bitcast_fusion.1) | copy-start | bytes 31108
  1117.9 3.4 collective-permute-start.16
  1119.2 5.5 collective-permute-start.17
  1124.8 9.9 collective-permute-start.18
  1130.7 6.9 collective-permute-start.19
  1148.6 54.1 %copy-start.1 = (bf16[16,4,128]{2,1,0:T(4,128)(2,1)S(1)}, bf16[16,4,128]{2,1,0:T(4,128)(2,1)}, u32[]{:S(2)}) copy-start(bf16[16,4,128]{2,1,0:T(4,128)(2,1)} %param.14) | copy-start | bytes 49156
  (59 other events, 536.1 us)
Sparse Core Ops, SparseCore 0:
  38.3 34.8 reduce-scatter.1
  164.3 548.9 all-reduce.16
  716.0 85.4 all-reduce.18
